TPU v7x, 512 devices: a whole 4x4x16 slice. The times are simulated.
512 devices in a mesh: lon: 16 (over z), lat: 8 (over x, y_lo), ens: 4 (over y_hi, core).
Axes of the slice: x: 4, y: 4 (y_hi: 2, y_lo: 2; y = y_hi * 2 + y_lo), z: 16, core: 2. Of those that a mesh axis runs over, the one named last changes fastest.
Arguments:
- field: bfloat16 [4, 128, 1024, 128], P('ens', 'lat', 'lon'), may hold values from -6 to 6
- cotangent: bfloat16 [4, 128, 1024, 128], P('ens', 'lat', 'lon'), may hold values from -6 to 6
- land_mask: int32 [128, 1024], P('lat', 'lon'), may hold values from 0 to 1, as said below
- kernel_taps: float32 [49, 128], replicated, may hold values from -0.875 to 0.875
- norm_gain: float32 [128], replicated, may hold values from 0.1 to 1.9
- norm_shift: float32 [128], replicated, may hold values from -3 to 3
- up_weight: bfloat16 [128, 256], replicated, may hold values from -0.5 to 0.5
- down_weight: bfloat16 [256, 128], replicated, may hold values from -0.375 to 0.375
Outputs:
- output: bfloat16 [4, 128, 1024, 128], P('ens', 'lat', 'lon')
- field_grad: bfloat16 [4, 128, 1024, 128], P('ens', 'lat', 'lon')
- kernel_grad: float32 [49, 128], replicated
- norm_grad: float32 [2, 128], replicated
- up_grad: float32 [128, 256], replicated
- down_grad: float32 [256, 128], replicated
Inputs may be any that keep to these rules, and one draw needn't show every extreme that they name: `land_mask`: 1 marks an ocean cell and 0 a land cell; the share of ocean differs from tile to tile.
All inputs are finite; a program needn't handle non-finite values.
Results may differ from a plain program's by a relative error of at most 0.0062.
Values may be sent and summed in bfloat16 or wider, within the bound.
A program may use at most 64 MiB of HBM per device.

v0:
```python
import math
import jax
import jax.numpy as jnp
from jax import lax
from jax.sharding import PartitionSpec as P

KERNEL = 7
DILATION = 2
REACH = 6


def partner(shard, axis, bit):
    return lax.ppermute(shard, axis, [(i, i ^ 1 << bit) for i in range(lax.axis_size(axis))])


def extended_2(cells, sides, width, closed):
    for axis, dim in sides:
        count = lax.axis_size(axis)
        ends = count if closed else count - 1
        head = lax.slice_in_dim(cells, 0, width, axis=dim)
        tail = lax.slice_in_dim(cells, cells.shape[dim] - width, cells.shape[dim], axis=dim)
        cells = jnp.concatenate(
            [
                lax.ppermute(tail, axis, [(i, (i + 1) % count) for i in range(ends)]),
                cells,
                lax.ppermute(head, axis, [((i + 1) % count, i) for i in range(ends)]),
            ],
            axis=dim,
        )
    return cells


def shifted(block, axis, distance):
    devices = range(lax.axis_size(axis))
    route = [((i - distance) % len(devices), i) for i in devices]
    return lax.ppermute(block, axis, route)


def passed_along(value, axis, steps):
    count = lax.axis_size(axis)
    leading, last = (max(0, -steps), min(count, count - steps))
    return lax.ppermute(value, axis, [(source, source + steps) for source in range(leading, last)])


def depthwise(widened, kernel_taps, rows, cols):
    total = jnp.zeros((rows, cols, widened.shape[2]), jnp.float32)
    for row_tap in range(KERNEL):
        for col_tap in range(KERNEL):
            window = widened[
                DILATION * row_tap : DILATION * row_tap + rows,
                DILATION * col_tap : DILATION * col_tap + cols,
            ]
            total = total + kernel_taps[row_tap * KERNEL + col_tap] * window
    return total


def fold_forward(strip):
    for bit_pos in range(lax.axis_size("lon").bit_length() - 1):
        strip = partner(strip, "lon", bit_pos)
    return strip


def fold_backward(strip):
    for bit_pos in range(lax.axis_size("lon").bit_length() - 1):
        strip = partner(strip.astype(jnp.bfloat16), "lon", bit_pos).astype(strip.dtype)
    return strip


def is_northern():
    return lax.axis_index("lat") == lax.axis_size("lat") - 1


def extend_rows(block):
    padded = extended_2(block, (("lat", 0),), REACH, False)
    height = block.shape[0]
    folded = fold_forward(block[height - REACH :][::-1, ::-1])
    upper = jnp.where(is_northern(), folded, padded[height + REACH :])
    return jnp.concatenate([padded[: height + REACH], upper], 0)


def extend_cols(block):
    return extended_2(block, (("lon", 1),), REACH, True)


def retract_cols(grads):
    width = grads.shape[1] - 2 * REACH
    own = grads[:, REACH : REACH + width]
    from_east = shifted(grads[:, :REACH].astype(jnp.bfloat16), "lon", -1).astype(jnp.float32)
    from_west = shifted(grads[:, REACH + width :].astype(jnp.bfloat16), "lon", 1).astype(
        jnp.float32
    )
    own = own.at[:, width - REACH :].add(from_east)
    return own.at[:, :REACH].add(from_west)


def retract_rows(grads):
    height = grads.shape[0] - 2 * REACH
    own = grads[REACH : REACH + height]
    upper = grads[REACH + height :]
    from_north = passed_along(grads[:REACH].astype(jnp.bfloat16), "lat", -1).astype(jnp.float32)
    from_south = passed_along(upper.astype(jnp.bfloat16), "lat", 1).astype(upper.dtype)
    folded = fold_backward(upper[::-1, ::-1])
    own = own.at[height - REACH :].add(from_north + jnp.where(is_northern(), folded, 0.0))
    return own.at[:REACH].add(from_south)


def shards(field, cotangent, land_mask, kernel_taps, norm_gain, norm_shift, up_weight, down_weight):
    state = field[0]
    upstream_in = cotangent[0]
    rows, cols, channels = state.shape
    sea = land_mask.astype(jnp.float32)[:, :, None]
    masked = (state.astype(jnp.float32) * sea).astype(jnp.bfloat16)
    extended = extend_cols(extend_rows(masked))
    widened = extended.astype(jnp.float32)
    mixed = depthwise(widened, kernel_taps, rows, cols)
    centered = mixed - jnp.mean(mixed, -1, keepdims=True)
    rstd = lax.rsqrt(jnp.mean(centered * centered, -1, keepdims=True) + 1e-06)
    unit = centered * rstd
    normed = (unit * norm_gain + norm_shift).astype(jnp.bfloat16)
    cells = rows * cols
    flat_norm = normed.reshape(cells, channels)
    pre = jnp.dot(flat_norm, up_weight, preferred_element_type=jnp.float32)
    slope = math.sqrt(2.0 / math.pi)
    tanh_val = jnp.tanh(slope * (pre + 0.044715 * pre * pre * pre))
    activated = (0.5 * pre * (1.0 + tanh_val)).astype(jnp.bfloat16)
    product = jnp.dot(activated, down_weight, preferred_element_type=jnp.float32).reshape(
        rows, cols, channels
    )
    output = ((state.astype(jnp.float32) + product) * sea).astype(jnp.bfloat16)
    upstream = (upstream_in.astype(jnp.float32) * sea).astype(jnp.bfloat16)
    flat_up = upstream.reshape(cells, channels)
    down_part = jnp.dot(activated.T, flat_up, preferred_element_type=jnp.float32)
    act_grad = jnp.dot(flat_up, down_weight.T, preferred_element_type=jnp.float32)
    deriv = 0.5 * (1.0 + tanh_val) + 0.5 * pre * (1.0 - tanh_val * tanh_val) * slope * (
        1.0 + 3.0 * 0.044715 * pre * pre
    )
    pre_grad = (act_grad * deriv).astype(jnp.bfloat16)
    up_part = jnp.dot(flat_norm.T, pre_grad, preferred_element_type=jnp.float32)
    norm_in_grad = jnp.dot(pre_grad, up_weight.T, preferred_element_type=jnp.float32).reshape(
        rows, cols, channels
    )
    norm_part = jnp.stack([jnp.sum(norm_in_grad * unit, (0, 1)), jnp.sum(norm_in_grad, (0, 1))])
    count = cells * lax.axis_size("lon") * lax.axis_size("lat") * lax.axis_size("ens")
    factor = 1.0 / math.sqrt(count)
    scaled = norm_in_grad * norm_gain
    mixed_grad = rstd * (
        scaled
        - jnp.mean(scaled, -1, keepdims=True)
        - unit * jnp.mean(scaled * unit, -1, keepdims=True)
    )
    kernel_rows = []
    for row_tap in range(KERNEL):
        for col_tap in range(KERNEL):
            window = widened[
                DILATION * row_tap : DILATION * row_tap + rows,
                DILATION * col_tap : DILATION * col_tap + cols,
            ]
            kernel_rows.append(jnp.sum(window * mixed_grad, (0, 1)))
    kernel_part = jnp.stack(kernel_rows)
    margin = 2 * REACH
    spread_grad = jnp.pad(mixed_grad, ((margin, margin), (margin, margin), (0, 0)))
    extended_grad = jnp.zeros((rows + margin, cols + margin, channels), jnp.float32)
    for row_tap in range(KERNEL):
        for col_tap in range(KERNEL):
            row_start = margin - DILATION * row_tap
            col_start = margin - DILATION * col_tap
            window = spread_grad[
                row_start : row_start + rows + margin, col_start : col_start + cols + margin
            ]
            extended_grad = extended_grad + kernel_taps[row_tap * KERNEL + col_tap] * window
    masked_grad = retract_rows(retract_cols(extended_grad))
    field_grad = ((upstream_in.astype(jnp.float32) + masked_grad) * sea).astype(jnp.bfloat16)
    kernel_sum, norm_sum, up_sum, down_sum = lax.psum(
        (kernel_part, norm_part, up_part, down_part), ("lon", "lat", "ens")
    )
    return (
        output[None],
        field_grad[None],
        kernel_sum * factor,
        norm_sum * factor,
        up_sum * factor,
        down_sum * factor,
    )


def solution(mesh):
    in_specs = (
        P("ens", "lat", "lon", None),
        P("ens", "lat", "lon", None),
        P("lat", "lon"),
        P(),
        P(),
        P(),
        P(),
        P(),
    )
    out_specs = (P("ens", "lat", "lon", None), P("ens", "lat", "lon", None), P(), P(), P(), P())
    return jax.shard_map(shards, mesh=mesh, in_specs=in_specs, out_specs=out_specs, check_vma=False)
```

profile of v0, /device:TPU:36, one launch (start us, length us, event | category | flops | bytes accessed | tf_op | source)
XLA Modules:
  0.0 698.0 jit_solution(13167900297526407773)
XLA Ops:
  7.2 0.0 copy-start
  7.2 0.0 copy-start.2
  7.2 0.0 all-reduce.5.cloned.1.call-start
  7.3 0.8 convert_element_type.87
  8.0 1.1 fusion.106
  9.2 2.0 collective-permute-start.1
  11.3 3.5 collective-permute-start
  14.7 3.3 collective-permute-start.5
  18.0 0.1 mul.1350
  18.1 0.0 collective-permute-done.1
  18.1 5.2 collective-permute-start.2
  23.3 0.2 fusion.107
  23.5 2.4 collective-permute-done.2
  25.9 9.1 %collective-permute-start.3 = (bf16[6,64,128]{2,1,0:T(8,128)(2,1)S(1)}, bf16[6,64,128]{2,1,0:T(8,128)(2,1)S(1)}, u32[]{:S(2)}, u32[]{:S(2)}) collective-permute-start(bf16[6,64,128]{2,1,0:T(8,128)(2,1)S(1)} %collective-permute-done.2), channel_id=1, source_target_pairs={{0,128},{32,160},{64,192},{96,224},{128,0},{160,32},{192,64},{224,... | collective-permute-start | bytes 294920 | tf_op jit(solution)/shard_map/ppermute | solution.py:13
  35.0 4.4 collective-permute-done.3
  39.4 14.6 %collective-permute-start.4 = (bf16[6,64,128]{2,1,0:T(8,128)(2,1)S(1)}, bf16[6,64,128]{2,1,0:T(8,128)(2,1)S(1)}, u32[]{:S(2)}, u32[]{:S(2)}) collective-permute-start(bf16[6,64,128]{2,1,0:T(8,128)(2,1)S(1)} %collective-permute-done.3), channel_id=1, source_target_pairs={{0,256},{32,288},{64,320},{96,352},{128,384},{160,416},{192,448},{... | collective-permute-start | bytes 294920 | tf_op jit(solution)/shard_map/ppermute | solution.py:13
  54.1 0.0 collective-permute-done.5
  54.1 5.7 collective-permute-done.4
  59.8 1.9 collective-permute-start.6
  61.8 3.9 collective-permute-start.7
  65.7 0.2 collective-permute-done.6
  65.9 1.9 collective-permute-done.7
  67.8 0.2 maximum_convert_fusion
  68.0 0.0 copy-start.6
  68.0 0.0 copy-start.7
  68.1 3.9 fusion.116
  72.0 0.4 multiply_reduce_fusion.52
  72.4 0.3 add_convert_fusion
  72.8 0.0 copy-start.4
  72.8 0.5 multiply_convert_fusion
  73.3 1.0 fusion.122
  74.3 0.3 fusion.120
  74.6 0.8 fusion
  75.4 0.9 fusion.121
  76.3 0.4 fusion.113
  76.7 0.1 div.17
  76.8 0.5 multiply_reduce_fusion
  77.3 1.5 multiply_reduce_fusion.1
  78.8 0.7 multiply_reduce_fusion.37
  79.5 0.9 multiply_reduce_fusion.19
  80.4 10.4 %fusion.114 = (bf16[28,76,128]{2,1,0:T(8,128)(2,1)S(1)}, f32[28,76,128]{2,1,0:T(8,128)S(1)}) fusion(f32[128]{0:T(128)S(1)} %get-tuple-element.172, f32[128]{0:T(128)S(1)} %get-tuple-element.173, f32[128]{0:T(128)S(1)} %get-tuple-element.126, f32[128]{0:T(128)S(1)} %get-tuple-element.127, f32[128]{0:T(128)S(1)} %get-tuple-element.128, ...), kind=kLoop, calls=%fused_computation.297 | loop fusion | flops 26693632 | bytes 2183680 | tf_op jit(solution)/shard_map/convert.5
  90.8 0.9 fusion.104
  91.8 2.8 collective-permute-start.9
  94.5 5.5 collective-permute-start.8
  100.1 0.1 slice.883
  100.2 0.1 stack.208
  100.3 102.3 %all-reduce.1 = (f32[49,128]{1,0:T(8,128)S(1)}, f32[2,128]{1,0:T(2,128)S(1)}) all-reduce(f32[49,128]{1,0:T(8,128)S(1)} %stack.208, f32[2,128]{1,0:T(2,128)S(1)} %pad_maximum_fusion.3), channel_id=1, replica_groups=mesh['lon'=16,'lat'=8,'ens'=4] {'lon','lat','ens'}, use_global_device_ids=true, to_apply=%region_53.54 | all-reduce | flops 6528 | bytes 52224 | tf_op jit(solution)/shard_map/psum | solution.py:173
  202.7 0.2 scatter-add.14
  202.9 0.2 scatter-add.15
  203.3 2.8 collective-permute-start.11
  206.0 0.6 broadcast_multiply_fusion.2
  206.6 0.0 all-reduce.5.cloned.1.call-update
  206.7 3.1 collective-permute-done.11
  209.8 3.5 collective-permute-start.12
  213.3 0.6 broadcast_multiply_fusion.6
  213.9 2.8 collective-permute-start.15
  216.7 4.1 collective-permute-start.10
  220.8 6.5 collective-permute-start.13
  227.3 440.4 %all-reduce.5.cloned.1.call-done = (f32[128,256]{1,0:T(8,128)}, f32[256,128]{1,0:T(8,128)}) async-done(((f32[128,256]{1,0:T(8,128)}, f32[256,128]{1,0:T(8,128)}), (f32[128,256]{1,0:T(8,128)}, f32[256,128]{1,0:T(8,128)})) %all-reduce.5.cloned.1.call-update) | async-done | bytes 262160 | tf_op jit(solution)/shard_map/psum | solution.py:173
  667.7 1.6 broadcast_multiply_fusion.1
  669.3 9.2 %collective-permute-start.14 = (bf16[6,64,128]{2,1,0:T(8,128)(2,1)S(1)}, bf16[6,64,128]{2,1,0:T(8,128)(2,1)S(1)}, u32[]{:S(2)}, u32[]{:S(2)}) collective-permute-start(bf16[6,64,128]{2,1,0:T(8,128)(2,1)S(1)} %collective-permute-done.13), channel_id=1, source_target_pairs={{0,256},{32,288},{64,320},{96,352},{128,384},{160,416},{192,448},{... | collective-permute-start | bytes 294920 | tf_op jit(solution)/shard_map/ppermute | solution.py:13
  678.4 1.6 broadcast_multiply_fusion
  680.0 10.2 %collective-permute-done.14 = bf16[6,64,128]{2,1,0:T(8,128)(2,1)S(1)} collective-permute-done((bf16[6,64,128]{2,1,0:T(8,128)(2,1)S(1)}, bf16[6,64,128]{2,1,0:T(8,128)(2,1)S(1)}, u32[]{:S(2)}, u32[]{:S(2)}) %collective-permute-start.14) | collective-permute-done | bytes 98336 | tf_op jit(solution)/shard_map/ppermute | solution.py:13
  690.3 0.9 fusion.110
  (38 shorter events, 0.5 us)
Async XLA Ops:
  7.2 65.6 %copy-start = (bf16[128,256]{1,0:T(8,128)(2,1)S(1)}, bf16[128,256]{1,0:T(8,128)(2,1)}, u32[]{:S(2)}) copy-start(bf16[128,256]{1,0:T(8,128)(2,1)} %param.22) | copy-start | bytes 196612
  7.2 16.1 %copy-start.2 = (bf16[1,16,64,128]{3,2,1,0:T(8,128)(2,1)S(1)}, bf16[1,16,64,128]{3,2,1,0:T(8,128)(2,1)}, u32[]{:S(2)}) copy-start(bf16[1,16,64,128]{3,2,1,0:T(8,128)(2,1)} %param.17) | copy-start | bytes 786436
  7.2 27.8 %copy-start.5 = (f32[49,128]{1,0:T(8,128)S(1)}, f32[49,128]{1,0:T(8,128)}, u32[]{:S(2)}) copy-start(f32[49,128]{1,0:T(8,128)} %param.19) | copy-start | bytes 75268
  7.2 660.5 %all-reduce.5.cloned.1.call-start = ((), (), s32[]{:S(2)}) async-start(), calls=%async_computation | async-start | bytes 524288 | tf_op jit(solution)/shard_map/psum | solution.py:173
  9.2 8.9 %collective-permute-start.1 = (bf16[6,64,128]{2,1,0:T(8,128)(2,1)S(1)}, bf16[6,64,128]{2,1,0:T(8,128)(2,1)S(1)}, u32[]{:S(2)}, u32[]{:S(2)}) collective-permute-start(bf16[6,64,128]{2,1,0:T(8,128)(2,1)S(1)} %rev.6), channel_id=1, source_target_pairs={{0,32},{32,0},{64,96},{96,64},{128,160},{160,128},{192,224},{224,1... | collective-permute-start | bytes 294920 | tf_op jit(solution)/shard_map/ppermute | solution.py:13
  11.3 48.5 %collective-permute-start = (bf16[6,64,128]{2,1,0:T(8,128)(2,1)S(1)}, bf16[6,64,128]{2,1,0:T(8,128)(2,1)S(1)}, u32[]{:S(2)}, u32[]{:S(2)}) collective-permute-start(bf16[6,64,128]{2,1,0:T(8,128)(2,1)S(1)} %get-tuple-element.124), channel_id=1, source_target_pairs={{0,4},{4,8},{8,12},{12,16},{16,20},{20,24},{24,28},{1,5},{5,9},{9,... | collective-permute-start | bytes 294920 | tf_op jit(solution)/shard_map/ppermute | solution.py:24
  14.7 39.3 %collective-permute-start.5 = (bf16[6,64,128]{2,1,0:T(8,128)(2,1)S(1)}, bf16[6,64,128]{2,1,0:T(8,128)(2,1)S(1)}, u32[]{:S(2)}, u32[]{:S(2)}) collective-permute-start(bf16[6,64,128]{2,1,0:T(8,128)(2,1)S(1)} %get-tuple-element.123), channel_id=1, source_target_pairs={{4,0},{8,4},{12,8},{16,12},{20,16},{24,20},{28,24},{5,1},{9,5},{13... | collective-permute-start | bytes 294920 | tf_op jit(solution)/shard_map/ppermute | solution.py:26
  18.1 7.8 %collective-permute-start.2 = (bf16[6,64,128]{2,1,0:T(8,128)(2,1)S(1)}, bf16[6,64,128]{2,1,0:T(8,128)(2,1)S(1)}, u32[]{:S(2)}, u32[]{:S(2)}) collective-permute-start(bf16[6,64,128]{2,1,0:T(8,128)(2,1)S(1)} %collective-permute-done.1), channel_id=1, source_target_pairs={{0,64},{32,96},{64,0},{96,32},{128,192},{160,224},{192,128},{224,1... | collective-permute-start | bytes 294920 | tf_op jit(solution)/shard_map/ppermute | solution.py:13
  25.9 13.5 %collective-permute-start.3 = (bf16[6,64,128]{2,1,0:T(8,128)(2,1)S(1)}, bf16[6,64,128]{2,1,0:T(8,128)(2,1)S(1)}, u32[]{:S(2)}, u32[]{:S(2)}) collective-permute-start(bf16[6,64,128]{2,1,0:T(8,128)(2,1)S(1)} %collective-permute-done.2), channel_id=1, source_target_pairs={{0,128},{32,160},{64,192},{96,224},{128,0},{160,32},{192,64},{224,... | collective-permute-start | bytes 294920 | tf_op jit(solution)/shard_map/ppermute | solution.py:13
  39.4 20.4 %collective-permute-start.4 = (bf16[6,64,128]{2,1,0:T(8,128)(2,1)S(1)}, bf16[6,64,128]{2,1,0:T(8,128)(2,1)S(1)}, u32[]{:S(2)}, u32[]{:S(2)}) collective-permute-start(bf16[6,64,128]{2,1,0:T(8,128)(2,1)S(1)} %collective-permute-done.3), channel_id=1, source_target_pairs={{0,256},{32,288},{64,320},{96,352},{128,384},{160,416},{192,448},{... | collective-permute-start | bytes 294920 | tf_op jit(solution)/shard_map/ppermute | solution.py:13
  59.8 6.1 collective-permute-start.6
  61.8 6.1 collective-permute-start.7
  68.0 4.4 copy-start.6
  68.0 4.4 copy-start.7
  72.8 1.5 copy-start.4
  80.4 10.5 %copy-start.1 = (bf16[1,16,64,128]{3,2,1,0:T(8,128)(2,1)S(1)}, bf16[1,16,64,128]{3,2,1,0:T(8,128)(2,1)}, u32[]{:S(2)}) copy-start(bf16[1,16,64,128]{3,2,1,0:T(8,128)(2,1)} %param.16) | copy-start | bytes 786436
  91.8 111.2 %collective-permute-start.9 = (bf16[28,6,128]{2,1,0:T(8,128)(2,1)S(1)}, bf16[28,6,128]{2,1,0:T(8,128)(2,1)S(1)}, u32[]{:S(2)}, u32[]{:S(2)}) collective-permute-start(bf16[28,6,128]{2,1,0:T(8,128)(2,1)S(1)} %get-tuple-element.119), channel_id=1, source_target_pairs={{480,0},{0,32},{32,64},{64,96},{96,128},{128,160},{160,192},{192,2... | collective-permute-start | bytes 129032 | tf_op jit(solution)/shard_map/ppermute | solution.py:36
  94.5 108.1 %collective-permute-start.8 = (bf16[28,6,128]{2,1,0:T(8,128)(2,1)S(1)}, bf16[28,6,128]{2,1,0:T(8,128)(2,1)S(1)}, u32[]{:S(2)}, u32[]{:S(2)}) collective-permute-start(bf16[28,6,128]{2,1,0:T(8,128)(2,1)S(1)} %get-tuple-element.120), channel_id=1, source_target_pairs={{32,0},{64,32},{96,64},{128,96},{160,128},{192,160},{224,192},{256... | collective-permute-start | bytes 129032 | tf_op jit(solution)/shard_map/ppermute | solution.py:36
  203.3 6.5 collective-permute-start.11
  209.8 11.0 %collective-permute-start.12 = (bf16[6,64,128]{2,1,0:T(8,128)(2,1)S(1)}, bf16[6,64,128]{2,1,0:T(8,128)(2,1)S(1)}, u32[]{:S(2)}, u32[]{:S(2)}) collective-permute-start(bf16[6,64,128]{2,1,0:T(8,128)(2,1)S(1)} %collective-permute-done.11), channel_id=1, source_target_pairs={{0,64},{32,96},{64,0},{96,32},{128,192},{160,224},{192,128},{224,1... | collective-permute-start | bytes 294920 | tf_op jit(solution)/shard_map/ppermute | solution.py:13
  213.8 476.4 %copy-start.3 = (bf16[1,16,64,128]{3,2,1,0:T(8,128)(2,1)S(1)}, bf16[1,16,64,128]{3,2,1,0:T(8,128)(2,1)}, u32[]{:S(2)}) copy-start(bf16[1,16,64,128]{3,2,1,0:T(8,128)(2,1)} %param.17) | copy-start | bytes 786436
  213.9 476.3 %collective-permute-start.15 = (bf16[6,64,128]{2,1,0:T(8,128)(2,1)S(1)}, bf16[6,64,128]{2,1,0:T(8,128)(2,1)S(1)}, u32[]{:S(2)}, u32[]{:S(2)}) collective-permute-start(bf16[6,64,128]{2,1,0:T(8,128)(2,1)S(1)} %get-tuple-element.116), channel_id=1, source_target_pairs={{0,4},{4,8},{8,12},{12,16},{16,20},{20,24},{24,28},{1,5},{5,9},{9,... | collective-permute-start | bytes 294920 | tf_op jit(solution)/shard_map/ppermute | solution.py:42
  216.7 463.3 %collective-permute-start.10 = (bf16[6,64,128]{2,1,0:T(8,128)(2,1)S(1)}, bf16[6,64,128]{2,1,0:T(8,128)(2,1)S(1)}, u32[]{:S(2)}, u32[]{:S(2)}) collective-permute-start(bf16[6,64,128]{2,1,0:T(8,128)(2,1)S(1)} %get-tuple-element.118), channel_id=1, source_target_pairs={{4,0},{8,4},{12,8},{16,12},{20,16},{24,20},{28,24},{5,1},{9,5},{13... | collective-permute-start | bytes 294920 | tf_op jit(solution)/shard_map/ppermute | solution.py:42
  220.8 448.5 %collective-permute-start.13 = (bf16[6,64,128]{2,1,0:T(8,128)(2,1)S(1)}, bf16[6,64,128]{2,1,0:T(8,128)(2,1)S(1)}, u32[]{:S(2)}, u32[]{:S(2)}) collective-permute-start(bf16[6,64,128]{2,1,0:T(8,128)(2,1)S(1)} %collective-permute-done.12), channel_id=1, source_target_pairs={{0,128},{32,160},{64,192},{96,224},{128,0},{160,32},{192,64},{224,... | collective-permute-start | bytes 294920 | tf_op jit(solution)/shard_map/ppermute | solution.py:13
  669.3 20.9 %collective-permute-start.14 = (bf16[6,64,128]{2,1,0:T(8,128)(2,1)S(1)}, bf16[6,64,128]{2,1,0:T(8,128)(2,1)S(1)}, u32[]{:S(2)}, u32[]{:S(2)}) collective-permute-start(bf16[6,64,128]{2,1,0:T(8,128)(2,1)S(1)} %collective-permute-done.13), channel_id=1, source_target_pairs={{0,256},{32,288},{64,320},{96,352},{128,384},{160,416},{192,448},{... | collective-permute-start | bytes 294920 | tf_op jit(solution)/shard_map/ppermute | solution.py:13
Sparse Core Ops, SparseCore 0:
  206.8 460.8 all-reduce.4
where the time goes:
time: 699 us; the launch traced here: 698 us
  waiting for transfers between devices  468 us (67%)
  blocking collectives  102 us (15%)
  starting transfers between devices  80.6 us (12%)
  other arithmetic  27.3 us (4%)
  between operations  14.5 us (2%)
    psum x1, waiting for transfers between devices, shards(): lax.psum((kernel_part, norm_part, up_part, down_part), ('lon', 'lat', 'en...  440 us
    psum x1, blocking collectives, shards(): lax.psum((kernel_part, norm_part, up_part, down_part), ('lon', 'lat', 'en...  102 us
    ppermute x8, starting transfers between devices, partner(): lax.ppermute(shard, axis, [(i, i ^ 1 << bit) for i in range(lax.axis_size...  52.8 us
    ppermute x8, waiting for transfers between devices, partner(): lax.ppermute(shard, axis, [(i, i ^ 1 << bit) for i in range(lax.axis_size...  25.8 us
  transfers between devices with their start and end apart: 17, of which 8 were waited for; matrix products, arithmetic and copies ran while one was open for 1% of the time, Pallas kernels for 0%

commit v1 on v0

--- a/solution.py
+++ b/solution.py
@@ -171,7 +171,7 @@
     masked_grad = retract_rows(retract_cols(extended_grad))
     field_grad = ((upstream_in.astype(jnp.float32) + masked_grad) * sea).astype(jnp.bfloat16)
     kernel_sum, norm_sum, up_sum, down_sum = lax.psum(
-        (kernel_part, norm_part, up_part, down_part), ("lon", "lat", "ens")
+        lax.psum((kernel_part, norm_part, up_part, down_part), "lon"), ("lat", "ens")
     )
     return (
         output[None],

time: 699 us -> 445 us (0.64)
  the two profiles are of different devices: /device:TPU:36 before, /device:TPU:1 now
where the time goes in v1:
time: 445 us; the launch traced here: 444 us
  blocking collectives  179 us (40%)
  waiting for transfers between devices  140 us (31%)
  starting transfers between devices  74.2 us (17%)
  other arithmetic  29.3 us (7%)
  between operations  15.2 us (3%)
    psum x1, blocking collectives, shards(): lax.psum(lax.psum((kernel_part, norm_part, up_part, down_part), 'lon'), (...  137 us
    psum x1, waiting for transfers between devices, shards(): lax.psum(lax.psum((kernel_part, norm_part, up_part, down_part), 'lon'), (...  119 us
    ppermute x8, starting transfers between devices, partner(): lax.ppermute(shard, axis, [(i, i ^ 1 << bit) for i in range(lax.axis_size...  50.8 us
    psum x1, blocking collectives, shards(): lax.psum((kernel_part, norm_part, up_part, down_part), 'lon')  42.1 us
    ppermute x8, waiting for transfers between devices, partner(): lax.ppermute(shard, axis, [(i, i ^ 1 << bit) for i in range(lax.axis_size...  18.2 us
    another operation x1, other arithmetic  10.3 us
  transfers between devices with their start and end apart: 18, of which 8 were waited for; matrix products, arithmetic and copies ran while one was open for 2% of the time, Pallas kernels for 0%

profile of v1, /device:TPU:1, one launch (start us, length us, event | category | flops | bytes accessed | tf_op | source)
XLA Modules:
  0.0 444.1 jit_solution(720135551529844497)
XLA Ops:
  7.2 0.0 copy-start
  7.2 0.0 all-reduce.10.cloned.1.call-start
  7.2 0.8 convert_element_type.87
  8.0 1.1 fusion.106
  9.2 4.4 collective-permute-start.1
  13.6 3.2 collective-permute-start
  16.8 1.3 collective-permute-start.5
  18.1 0.1 mul.1350
  18.2 4.9 %collective-permute-start.2 = (bf16[6,64,128]{2,1,0:T(8,128)(2,1)S(1)}, bf16[6,64,128]{2,1,0:T(8,128)(2,1)S(1)}, u32[]{:S(2)}, u32[]{:S(2)}) collective-permute-start(bf16[6,64,128]{2,1,0:T(8,128)(2,1)S(1)} %collective-permute-done.1), channel_id=1, source_target_pairs={{0,64},{32,96},{64,0},{96,32},{128,192},{160,224},{192,128},{224,1... | collective-permute-start | bytes 294920 | tf_op jit(solution)/shard_map/ppermute | solution.py:13
  23.1 0.2 fusion.107
  23.3 2.6 collective-permute-done.2
  25.9 11.0 %collective-permute-start.3 = (bf16[6,64,128]{2,1,0:T(8,128)(2,1)S(1)}, bf16[6,64,128]{2,1,0:T(8,128)(2,1)S(1)}, u32[]{:S(2)}, u32[]{:S(2)}) collective-permute-start(bf16[6,64,128]{2,1,0:T(8,128)(2,1)S(1)} %collective-permute-done.2), channel_id=1, source_target_pairs={{0,128},{32,160},{64,192},{96,224},{128,0},{160,32},{192,64},{224,... | collective-permute-start | bytes 294920 | tf_op jit(solution)/shard_map/ppermute | solution.py:13
  36.9 7.3 %collective-permute-done.3 = bf16[6,64,128]{2,1,0:T(8,128)(2,1)S(1)} collective-permute-done((bf16[6,64,128]{2,1,0:T(8,128)(2,1)S(1)}, bf16[6,64,128]{2,1,0:T(8,128)(2,1)S(1)}, u32[]{:S(2)}, u32[]{:S(2)}) %collective-permute-start.3) | collective-permute-done | bytes 98336 | tf_op jit(solution)/shard_map/ppermute | solution.py:13
  44.2 11.7 %collective-permute-start.4 = (bf16[6,64,128]{2,1,0:T(8,128)(2,1)S(1)}, bf16[6,64,128]{2,1,0:T(8,128)(2,1)S(1)}, u32[]{:S(2)}, u32[]{:S(2)}) collective-permute-start(bf16[6,64,128]{2,1,0:T(8,128)(2,1)S(1)} %collective-permute-done.3), channel_id=1, source_target_pairs={{0,256},{32,288},{64,320},{96,352},{128,384},{160,416},{192,448},{... | collective-permute-start | bytes 294920 | tf_op jit(solution)/shard_map/ppermute | solution.py:13
  56.0 2.5 collective-permute-done.4
  58.5 1.9 collective-permute-start.6
  60.4 7.2 %collective-permute-start.7 = (bf16[28,6,128]{2,1,0:T(8,128)(2,1)S(1)}, bf16[28,6,128]{2,1,0:T(8,128)(2,1)S(1)}, u32[]{:S(2)}, u32[]{:S(2)}) collective-permute-start(bf16[28,6,128]{2,1,0:T(8,128)(2,1)S(1)} %get-tuple-element.126), channel_id=1, source_target_pairs={{32,0},{64,32},{96,64},{128,96},{160,128},{192,160},{224,192},{256... | collective-permute-start | bytes 129032 | tf_op jit(solution)/shard_map/ppermute | solution.py:26
  67.7 1.2 collective-permute-done.7
  68.9 0.2 maximum_convert_fusion
  69.1 0.0 copy-start.8
  69.1 3.9 fusion.116
  73.1 0.4 multiply_reduce_fusion.52
  73.5 0.3 add_convert_fusion
  73.9 0.5 multiply_convert_fusion
  74.4 0.2 copy-done.1
  74.6 1.0 fusion.122
  75.6 0.3 fusion.120
  75.9 0.8 fusion
  76.6 0.4 fusion.113
  77.1 0.1 div.17
  77.1 0.9 multiply_reduce_fusion
  78.0 2.1 multiply_reduce_fusion.1
  80.1 1.2 multiply_reduce_fusion.37
  81.3 1.5 multiply_reduce_fusion.19
  82.9 10.3 %fusion.114 = (bf16[28,76,128]{2,1,0:T(8,128)(2,1)S(1)}, f32[28,76,128]{2,1,0:T(8,128)S(1)}) fusion(f32[128]{0:T(128)S(1)} %get-tuple-element.176, f32[128]{0:T(128)S(1)} %get-tuple-element.177, f32[128]{0:T(128)S(1)} %get-tuple-element.130, f32[128]{0:T(128)S(1)} %get-tuple-element.131, f32[128]{0:T(128)S(1)} %get-tuple-element.132, ...), kind=kLoop, calls=%fused_computation.297 | loop fusion | flops 26693632 | bytes 2183680 | tf_op jit(solution)/shard_map/convert.5
  93.2 0.9 fusion.104
  94.2 5.1 %collective-permute-start.8 = (bf16[28,6,128]{2,1,0:T(8,128)(2,1)S(1)}, bf16[28,6,128]{2,1,0:T(8,128)(2,1)S(1)}, u32[]{:S(2)}, u32[]{:S(2)}) collective-permute-start(bf16[28,6,128]{2,1,0:T(8,128)(2,1)S(1)} %get-tuple-element.124), channel_id=1, source_target_pairs={{32,0},{64,32},{96,64},{128,96},{160,128},{192,160},{224,192},{256... | collective-permute-start | bytes 129032 | tf_op jit(solution)/shard_map/ppermute | solution.py:36
  99.2 0.9 fusion.121
  100.5 1.9 collective-permute-start.9
  102.5 0.1 slice.883
  102.6 0.0 all-reduce.10.cloned.1.call-update
  102.6 0.0 all-reduce.8.cloned.1.call-start
  103.1 1.5 stack.208
  104.6 0.2 scatter-add.14
  104.8 1.9 collective-permute-done.9
  106.7 0.2 scatter-add.15
  107.0 1.9 collective-permute-start.11
  109.0 42.1 %all-reduce.3 = (f32[49,128]{1,0:T(8,128)S(1)}, f32[2,128]{1,0:T(2,128)S(1)}) all-reduce(f32[49,128]{1,0:T(8,128)S(1)} %stack.208, f32[2,128]{1,0:T(2,128)S(1)} %pad_maximum_fusion.3), channel_id=1, replica_groups=mesh['lon'=16,'lat'=8,'ens'=4] {'lon'}, use_global_device_ids=true, to_apply=%region_53.54 | all-reduce | flops 6528 | bytes 52224 | tf_op jit(solution)/shard_map/psum | solution.py:174
  151.1 136.7 %all-reduce.1 = (f32[49,128]{1,0:T(8,128)S(1)}, f32[2,128]{1,0:T(2,128)S(1)}) all-reduce(f32[49,128]{1,0:T(8,128)S(1)} %get-tuple-element.111, f32[2,128]{1,0:T(2,128)S(1)} %get-tuple-element.112), channel_id=1, replica_groups=mesh['lon'=16,'lat'=8,'ens'=4] {'lat','ens'}, use_global_device_ids=true, to_apply=%region_54.55 | all-reduce | flops 6528 | bytes 52224 | tf_op jit(solution)/shard_map/psum | solution.py:173
  287.8 2.0 collective-permute-start.12
  289.8 0.6 broadcast_multiply_fusion.2
  290.4 3.6 collective-permute-done.12
  294.1 5.5 %collective-permute-start.13 = (bf16[6,64,128]{2,1,0:T(8,128)(2,1)S(1)}, bf16[6,64,128]{2,1,0:T(8,128)(2,1)S(1)}, u32[]{:S(2)}, u32[]{:S(2)}) collective-permute-start(bf16[6,64,128]{2,1,0:T(8,128)(2,1)S(1)} %collective-permute-done.12), channel_id=1, source_target_pairs={{0,128},{32,160},{64,192},{96,224},{128,0},{160,32},{192,64},{224,... | collective-permute-start | bytes 294920 | tf_op jit(solution)/shard_map/ppermute | solution.py:13
  299.6 0.0 all-reduce.10.cloned.1.call-done
  299.6 0.0 all-reduce.8.cloned.1.call-update
  299.7 0.6 broadcast_multiply_fusion.6
  300.3 1.4 collective-permute-start.15
  301.7 1.3 collective-permute-start.10
  303.0 2.2 collective-permute-done.13
  305.2 9.3 %collective-permute-start.14 = (bf16[6,64,128]{2,1,0:T(8,128)(2,1)S(1)}, bf16[6,64,128]{2,1,0:T(8,128)(2,1)S(1)}, u32[]{:S(2)}, u32[]{:S(2)}) collective-permute-start(bf16[6,64,128]{2,1,0:T(8,128)(2,1)S(1)} %collective-permute-done.13), channel_id=1, source_target_pairs={{0,256},{32,288},{64,320},{96,352},{128,384},{160,416},{192,448},{... | collective-permute-start | bytes 294920 | tf_op jit(solution)/shard_map/ppermute | solution.py:13
  314.5 118.5 %all-reduce.8.cloned.1.call-done = (f32[128,256]{1,0:T(8,128)}, f32[256,128]{1,0:T(8,128)}) async-done(((f32[128,256]{1,0:T(8,128)}, f32[256,128]{1,0:T(8,128)}), (f32[128,256]{1,0:T(8,128)}, f32[256,128]{1,0:T(8,128)})) %all-reduce.8.cloned.1.call-update) | async-done | bytes 262160 | tf_op jit(solution)/shard_map/psum | solution.py:173
  433.1 1.6 broadcast_multiply_fusion.1
  434.7 1.6 broadcast_multiply_fusion
  436.4 0.9 fusion.110
  (128 shorter events, 0.7 us)
Async XLA Ops:
  7.2 66.7 %copy-start = (bf16[128,256]{1,0:T(8,128)(2,1)S(1)}, bf16[128,256]{1,0:T(8,128)(2,1)}, u32[]{:S(2)}) copy-start(bf16[128,256]{1,0:T(8,128)(2,1)} %param.22) | copy-start | bytes 196612
  7.2 15.9 %copy-start.4 = (bf16[1,16,64,128]{3,2,1,0:T(8,128)(2,1)S(1)}, bf16[1,16,64,128]{3,2,1,0:T(8,128)(2,1)}, u32[]{:S(2)}) copy-start(bf16[1,16,64,128]{3,2,1,0:T(8,128)(2,1)} %param.17) | copy-start | bytes 786436
  7.2 29.7 %copy-start.7 = (f32[49,128]{1,0:T(8,128)S(1)}, f32[49,128]{1,0:T(8,128)}, u32[]{:S(2)}) copy-start(f32[49,128]{1,0:T(8,128)} %param.19) | copy-start | bytes 75268
  7.2 292.4 %all-reduce.10.cloned.1.call-start = ((), (), s32[]{:S(2)}) async-start(), calls=%async_computation.1 | async-start | bytes 524288 | tf_op jit(solution)/shard_map/psum | solution.py:174
  9.2 9.0 %collective-permute-start.1 = (bf16[6,64,128]{2,1,0:T(8,128)(2,1)S(1)}, bf16[6,64,128]{2,1,0:T(8,128)(2,1)S(1)}, u32[]{:S(2)}, u32[]{:S(2)}) collective-permute-start(bf16[6,64,128]{2,1,0:T(8,128)(2,1)S(1)} %rev.6), channel_id=1, source_target_pairs={{0,32},{32,0},{64,96},{96,64},{128,160},{160,128},{192,224},{224,1... | collective-permute-start | bytes 294920 | tf_op jit(solution)/shard_map/ppermute | solution.py:13
  13.6 44.9 %collective-permute-start = (bf16[6,64,128]{2,1,0:T(8,128)(2,1)S(1)}, bf16[6,64,128]{2,1,0:T(8,128)(2,1)S(1)}, u32[]{:S(2)}, u32[]{:S(2)}) collective-permute-start(bf16[6,64,128]{2,1,0:T(8,128)(2,1)S(1)} %get-tuple-element.128), channel_id=1, source_target_pairs={{0,4},{4,8},{8,12},{12,16},{16,20},{20,24},{24,28},{1,5},{5,9},{9,... | collective-permute-start | bytes 294920 | tf_op jit(solution)/shard_map/ppermute | solution.py:24
  16.8 39.1 %collective-permute-start.5 = (bf16[6,64,128]{2,1,0:T(8,128)(2,1)S(1)}, bf16[6,64,128]{2,1,0:T(8,128)(2,1)S(1)}, u32[]{:S(2)}, u32[]{:S(2)}) collective-permute-start(bf16[6,64,128]{2,1,0:T(8,128)(2,1)S(1)} %get-tuple-element.127), channel_id=1, source_target_pairs={{4,0},{8,4},{12,8},{16,12},{20,16},{24,20},{28,24},{5,1},{9,5},{13... | collective-permute-start | bytes 294920 | tf_op jit(solution)/shard_map/ppermute | solution.py:26
  18.2 7.7 %collective-permute-start.2 = (bf16[6,64,128]{2,1,0:T(8,128)(2,1)S(1)}, bf16[6,64,128]{2,1,0:T(8,128)(2,1)S(1)}, u32[]{:S(2)}, u32[]{:S(2)}) collective-permute-start(bf16[6,64,128]{2,1,0:T(8,128)(2,1)S(1)} %collective-permute-done.1), channel_id=1, source_target_pairs={{0,64},{32,96},{64,0},{96,32},{128,192},{160,224},{192,128},{224,1... | collective-permute-start | bytes 294920 | tf_op jit(solution)/shard_map/ppermute | solution.py:13
  25.9 18.3 %collective-permute-start.3 = (bf16[6,64,128]{2,1,0:T(8,128)(2,1)S(1)}, bf16[6,64,128]{2,1,0:T(8,128)(2,1)S(1)}, u32[]{:S(2)}, u32[]{:S(2)}) collective-permute-start(bf16[6,64,128]{2,1,0:T(8,128)(2,1)S(1)} %collective-permute-done.2), channel_id=1, source_target_pairs={{0,128},{32,160},{64,192},{96,224},{128,0},{160,32},{192,64},{224,... | collective-permute-start | bytes 294920 | tf_op jit(solution)/shard_map/ppermute | solution.py:13
  44.2 14.3 %collective-permute-start.4 = (bf16[6,64,128]{2,1,0:T(8,128)(2,1)S(1)}, bf16[6,64,128]{2,1,0:T(8,128)(2,1)S(1)}, u32[]{:S(2)}, u32[]{:S(2)}) collective-permute-start(bf16[6,64,128]{2,1,0:T(8,128)(2,1)S(1)} %collective-permute-done.3), channel_id=1, source_target_pairs={{0,256},{32,288},{64,320},{96,352},{128,384},{160,416},{192,448},{... | collective-permute-start | bytes 294920 | tf_op jit(solution)/shard_map/ppermute | solution.py:13
  58.5 9.2 %collective-permute-start.6 = (bf16[28,6,128]{2,1,0:T(8,128)(2,1)S(1)}, bf16[28,6,128]{2,1,0:T(8,128)(2,1)S(1)}, u32[]{:S(2)}, u32[]{:S(2)}) collective-permute-start(bf16[28,6,128]{2,1,0:T(8,128)(2,1)S(1)} %get-tuple-element.125), channel_id=1, source_target_pairs={{0,32},{32,64},{64,96},{96,128},{128,160},{160,192},{192,224},{224... | collective-permute-start | bytes 129032 | tf_op jit(solution)/shard_map/ppermute | solution.py:24
  60.4 8.5 %collective-permute-start.7 = (bf16[28,6,128]{2,1,0:T(8,128)(2,1)S(1)}, bf16[28,6,128]{2,1,0:T(8,128)(2,1)S(1)}, u32[]{:S(2)}, u32[]{:S(2)}) collective-permute-start(bf16[28,6,128]{2,1,0:T(8,128)(2,1)S(1)} %get-tuple-element.126), channel_id=1, source_target_pairs={{32,0},{64,32},{96,64},{128,96},{160,128},{192,160},{224,192},{256... | collective-permute-start | bytes 129032 | tf_op jit(solution)/shard_map/ppermute | solution.py:26
  69.1 4.4 copy-start.8
  69.1 4.4 copy-start.50
  82.8 10.4 %copy-start.3 = (bf16[1,16,64,128]{3,2,1,0:T(8,128)(2,1)S(1)}, bf16[1,16,64,128]{3,2,1,0:T(8,128)(2,1)}, u32[]{:S(2)}) copy-start(bf16[1,16,64,128]{3,2,1,0:T(8,128)(2,1)} %param.16) | copy-start | bytes 786436
  93.2 6.0 %copy-start.2 = (bf16[16,64,128]{2,1,0:T(8,128)(2,1)S(1)}, bf16[16,64,128]{2,1,0:T(8,128)(2,1)}, u32[]{:S(2)}) copy-start(bf16[16,64,128]{2,1,0:T(8,128)(2,1)} %copy-done.1) | copy-start | bytes 786436
  94.2 10.4 %collective-permute-start.8 = (bf16[28,6,128]{2,1,0:T(8,128)(2,1)S(1)}, bf16[28,6,128]{2,1,0:T(8,128)(2,1)S(1)}, u32[]{:S(2)}, u32[]{:S(2)}) collective-permute-start(bf16[28,6,128]{2,1,0:T(8,128)(2,1)S(1)} %get-tuple-element.124), channel_id=1, source_target_pairs={{32,0},{64,32},{96,64},{128,96},{160,128},{192,160},{224,192},{256... | collective-permute-start | bytes 129032 | tf_op jit(solution)/shard_map/ppermute | solution.py:36
  100.2 2.5 copy-start.12
  100.2 2.5 copy-start.13
  100.2 2.5 copy-start.14
  100.2 2.5 copy-start.15
  100.2 2.5 copy-start.16
  100.2 2.5 copy-start.17
  100.2 2.5 copy-start.18
  100.2 2.5 copy-start.19
  100.3 2.5 copy-start.20
  100.3 2.5 copy-start.21
  100.3 2.5 copy-start.22
  100.3 2.5 copy-start.23
  100.3 2.5 copy-start.24
  100.3 2.5 copy-start.25
  100.3 2.5 copy-start.26
  100.3 2.5 copy-start.27
  100.3 2.5 copy-start.28
  100.3 2.5 copy-start.29
  100.4 2.5 copy-start.30
  100.4 2.5 copy-start.31
  100.4 2.5 copy-start.32
  100.4 2.5 copy-start.33
  100.4 2.5 copy-start.34
  100.4 2.5 copy-start.35
  100.4 2.5 copy-start.36
  100.4 2.5 copy-start.37
  100.4 2.5 copy-start.38
  100.4 2.5 copy-start.39
  100.5 2.5 copy-start.40
  100.5 2.5 copy-start.41
  100.5 2.5 copy-start.42
  100.5 2.5 copy-start.43
  100.5 2.5 copy-start.44
  100.5 2.5 copy-start.45
  100.5 2.5 copy-start.46
  100.5 2.5 copy-start.47
  100.5 2.5 copy-start.48
  100.5 6.1 %collective-permute-start.9 = (bf16[28,6,128]{2,1,0:T(8,128)(2,1)S(1)}, bf16[28,6,128]{2,1,0:T(8,128)(2,1)S(1)}, u32[]{:S(2)}, u32[]{:S(2)}) collective-permute-start(bf16[28,6,128]{2,1,0:T(8,128)(2,1)S(1)} %get-tuple-element.123), channel_id=1, source_target_pairs={{480,0},{0,32},{32,64},{64,96},{96,128},{128,160},{160,192},{192,2... | collective-permute-start | bytes 129032 | tf_op jit(solution)/shard_map/ppermute | solution.py:36
  102.6 330.5 %all-reduce.8.cloned.1.call-start = ((), (), s32[]{:S(2)}) async-start(), calls=%async_computation | async-start | bytes 524288 | tf_op jit(solution)/shard_map/psum | solution.py:173
  104.5 4.4 copy-start.49
  107.0 180.8 %collective-permute-start.11 = (bf16[6,64,128]{2,1,0:T(8,128)(2,1)S(1)}, bf16[6,64,128]{2,1,0:T(8,128)(2,1)S(1)}, u32[]{:S(2)}, u32[]{:S(2)}) collective-permute-start(bf16[6,64,128]{2,1,0:T(8,128)(2,1)S(1)} %rev.7), channel_id=1, source_target_pairs={{0,32},{32,0},{64,96},{96,64},{128,160},{160,128},{192,224},{224,1... | collective-permute-start | bytes 294920 | tf_op jit(solution)/shard_map/ppermute | solution.py:13
  287.8 6.2 %collective-permute-start.12 = (bf16[6,64,128]{2,1,0:T(8,128)(2,1)S(1)}, bf16[6,64,128]{2,1,0:T(8,128)(2,1)S(1)}, u32[]{:S(2)}, u32[]{:S(2)}) collective-permute-start(bf16[6,64,128]{2,1,0:T(8,128)(2,1)S(1)} %collective-permute-done.11), channel_id=1, source_target_pairs={{0,64},{32,96},{64,0},{96,32},{128,192},{160,224},{192,128},{224,1... | collective-permute-start | bytes 294920 | tf_op jit(solution)/shard_map/ppermute | solution.py:13
  294.1 11.1 %collective-permute-start.13 = (bf16[6,64,128]{2,1,0:T(8,128)(2,1)S(1)}, bf16[6,64,128]{2,1,0:T(8,128)(2,1)S(1)}, u32[]{:S(2)}, u32[]{:S(2)}) collective-permute-start(bf16[6,64,128]{2,1,0:T(8,128)(2,1)S(1)} %collective-permute-done.12), channel_id=1, source_target_pairs={{0,128},{32,160},{64,192},{96,224},{128,0},{160,32},{192,64},{224,... | collective-permute-start | bytes 294920 | tf_op jit(solution)/shard_map/ppermute | solution.py:13
  300.2 136.1 %copy-start.5 = (bf16[1,16,64,128]{3,2,1,0:T(8,128)(2,1)S(1)}, bf16[1,16,64,128]{3,2,1,0:T(8,128)(2,1)}, u32[]{:S(2)}) copy-start(bf16[1,16,64,128]{3,2,1,0:T(8,128)(2,1)} %param.17) | copy-start | bytes 786436
  300.3 136.0 %collective-permute-start.15 = (bf16[6,64,128]{2,1,0:T(8,128)(2,1)S(1)}, bf16[6,64,128]{2,1,0:T(8,128)(2,1)S(1)}, u32[]{:S(2)}, u32[]{:S(2)}) collective-permute-start(bf16[6,64,128]{2,1,0:T(8,128)(2,1)S(1)} %get-tuple-element.120), channel_id=1, source_target_pairs={{0,4},{4,8},{8,12},{12,16},{16,20},{20,24},{24,28},{1,5},{5,9},{9,... | collective-permute-start | bytes 294920 | tf_op jit(solution)/shard_map/ppermute | solution.py:42
  301.7 134.5 %collective-permute-start.10 = (bf16[6,64,128]{2,1,0:T(8,128)(2,1)S(1)}, bf16[6,64,128]{2,1,0:T(8,128)(2,1)S(1)}, u32[]{:S(2)}, u32[]{:S(2)}) collective-permute-start(bf16[6,64,128]{2,1,0:T(8,128)(2,1)S(1)} %get-tuple-element.122), channel_id=1, source_target_pairs={{4,0},{8,4},{12,8},{16,12},{20,16},{24,20},{28,24},{5,1},{9,5},{13... | collective-permute-start | bytes 294920 | tf_op jit(solution)/shard_map/ppermute | solution.py:42
  305.2 131.0 %collective-permute-start.14 = (bf16[6,64,128]{2,1,0:T(8,128)(2,1)S(1)}, bf16[6,64,128]{2,1,0:T(8,128)(2,1)S(1)}, u32[]{:S(2)}, u32[]{:S(2)}) collective-permute-start(bf16[6,64,128]{2,1,0:T(8,128)(2,1)S(1)} %collective-permute-done.13), channel_id=1, source_target_pairs={{0,256},{32,288},{64,320},{96,352},{128,384},{160,416},{192,448},{... | collective-permute-start | bytes 294920 | tf_op jit(solution)/shard_map/ppermute | solution.py:13
  (5 other events, 9.9 us)
Sparse Core Ops, SparseCore 0:
  102.7 131.1 all-reduce.9
  299.8 133.2 all-reduce.7
